TPU v7x, 32 devices: a whole 2x2x4 slice. The times are simulated.
32 devices in a mesh: groups: 2 (over y), seq: 4 (over z), mp: 2 (over x), section: 2 (over core).
Axes of the slice: x: 2, y: 2, z: 4, core: 2. Of those that a mesh axis runs over, the one named last changes fastest.
Arguments:
- features: bfloat16 [4, 512, 8192], P(('groups', 'section'), 'mp', 'seq'), parts along dimension 0, may hold values from -6 to 6
- alpha: float32 [512], P('mp'), may hold values from 0.5 to 2
- conv_weight: bfloat16 [1024, 32, 16], P('mp'), may hold values from -0.25 to 0.25
- qkv_weight: bfloat16 [1024, 3, 1024], P(None, None, 'mp'), may hold values from -1 to 1
- readout: float32 [1024], P('mp'), may hold values from -4 to 4
- offsets: int32 [4], P(('groups', 'section')), parts along dimension 0, may hold values from 0 to 14479
- pairs: int32 [8, 2], P('groups'), parts along dimension 0, may hold values from 0 to 1
- labels: int32 [8], P('groups'), parts along dimension 0, may hold values from 0 to 1
Outputs:
- grads: bfloat16 [3, 4, 1024, 1024], P(None, ('groups', 'section'), 'seq', 'mp'), parts along dimension 1
- rewards: float32 [4], P('groups'), parts along dimension 0
- loss: float32 [2], P('groups'), parts along dimension 0
There are 2 independent parts, one for each index of `groups`. A program takes and returns all parts, laid end to end along the dimension named above; an argument that names none is the same for every part. Nothing has to cross between parts.
All inputs are finite; a program needn't handle non-finite values.
Results may differ from a plain program's by a relative error of at most 0.017.
Values may be sent and summed in bfloat16 or wider, within the bound.
A program may use at most 64 MiB of HBM per device.

v0:
```python
import math

import jax
import jax.numpy as jnp
from jax import lax
from jax.sharding import PartitionSpec as P

D = 1024
HD = 64


EPS = 1e-06
BASE = 10000.0


def padded_2(block, sides, width):
    for axis, dim in sides:
        count = lax.axis_size(axis)
        forward = [(i, i + 1) for i in range(count - 1)]
        backward = [(target, source) for source, target in forward]
        low = lax.ppermute(
            lax.slice_in_dim(block, block.shape[dim] - width, None, axis=dim), axis, forward
        )
        high = lax.ppermute(lax.slice_in_dim(block, 0, width, axis=dim), axis, backward)
        block = jnp.concatenate([low, block, high], axis=dim)
    return block


def position_table(positions, feature_ids, width):
    pair_ids = (feature_ids // 2).astype(jnp.float32)
    freqs = jnp.exp(pair_ids * (-2.0 * math.log(BASE) / width))
    angle = positions.astype(jnp.float32)[..., None] * freqs
    return jnp.where(feature_ids % 2 == 0, jnp.sin(angle), jnp.cos(angle))


def local(features, alpha, conv_weight, qkv_weight, readout, offsets, pairs, labels):
    f32 = jnp.float32
    bf16 = jnp.bfloat16
    cand, chans, samples = features.shape
    local_width = conv_weight.shape[0]
    per_group = conv_weight.shape[1]
    kern = conv_weight.shape[2]
    stride = kern // 2
    frames_dev = samples // stride
    groups_here = chans // per_group
    heads_here = local_width // HD
    raw = features.astype(f32)
    slope = alpha[None, :, None]
    act = (raw + jnp.sin(slope * raw) ** 2 / slope).astype(bf16)
    padded = padded_2(act, (("seq", 2),), stride // 2)
    blocks = padded.reshape(cand, groups_here, per_group, frames_dev + 1, stride).transpose(
        0, 1, 3, 2, 4
    )
    patches = jnp.concatenate([blocks[:, :, :-1], blocks[:, :, 1:]], axis=-1).reshape(
        cand, groups_here, frames_dev, per_group * kern
    )
    kernel = conv_weight.reshape(groups_here, local_width // groups_here, per_group * kern)
    frames = jnp.einsum("cgfk,gok->cfgo", patches, kernel, preferred_element_type=f32).reshape(
        cand, frames_dev, local_width
    )
    slice_id = lax.axis_index("seq")
    part_id = lax.axis_index("mp")
    positions = (
        offsets[:, None] + slice_id * frames_dev + jnp.arange(frames_dev, dtype=jnp.int32)[None, :]
    )
    feature_ids = part_id * local_width + jnp.arange(local_width, dtype=jnp.int32)
    resid = (frames + position_table(positions, feature_ids, D)).astype(bf16)
    whole = lax.all_gather(resid, "mp", axis=2, tiled=True)
    squares = jnp.mean(jnp.square(whole.astype(f32)), axis=-1)
    projected = jnp.einsum("cfd,dtk->cftk", whole, qkv_weight, preferred_element_type=f32)
    qkv = (projected * lax.rsqrt(squares + EPS)[:, :, None, None]).astype(bf16)
    query = qkv[:, :, 0]
    keys, values = (
        lax.all_gather(qkv[:, :, 1], "seq", axis=1, tiled=True),
        lax.all_gather(qkv[:, :, 2], "seq", axis=1, tiled=True),
    )
    total = keys.shape[1]
    block = min(512, total)
    count_blocks = total // block
    scale = 1.0 / math.sqrt(HD)
    query4 = query.reshape(cand, frames_dev, heads_here, HD)

    def key_slice(source, start, size):
        return lax.dynamic_slice_in_dim(source, start, size, 1).reshape(cand, size, heads_here, HD)

    def scores_for(start, size):
        return (
            jnp.einsum(
                "cfhe,ckhe->chfk", query4, key_slice(keys, start, size), preferred_element_type=f32
            )
            * scale
        )

    def stat_step(carry, index):
        peak_now, mass_now = carry
        score = scores_for(index * block, block)
        fresh = jnp.maximum(peak_now, jnp.max(score, axis=-1))
        mass_now = mass_now * jnp.exp(peak_now - fresh) + jnp.sum(
            jnp.exp(score - fresh[..., None]), axis=-1
        )
        return ((fresh, mass_now), None)

    start_peak = jnp.full((cand, heads_here, frames_dev), -jnp.inf, f32)
    (peak, mass), _ = lax.scan(
        stat_step, (start_peak, jnp.zeros_like(start_peak)), jnp.arange(count_blocks)
    )

    def weights_for(start, size):
        return jnp.exp(scores_for(start, size) - peak[..., None]) / mass[..., None]

    def out_step(running, index):
        start = index * block
        prob = weights_for(start, block).astype(bf16)
        running = running + jnp.einsum(
            "chfk,ckhe->cfhe", prob, key_slice(values, start, block), preferred_element_type=f32
        )
        return (running, None)

    attended4, _ = lax.scan(
        out_step, jnp.zeros((cand, frames_dev, heads_here, HD), f32), jnp.arange(count_blocks)
    )
    attended = attended4.reshape(cand, frames_dev, local_width)
    gate = jax.nn.sigmoid(lax.optimization_barrier(resid).astype(f32))
    section_id = lax.axis_index("section")
    all_cands = cand * lax.axis_size("section")
    owner = (
        jnp.arange(all_cands, dtype=jnp.int32)[None, :]
        == (section_id * cand + jnp.arange(cand, dtype=jnp.int32))[:, None]
    ).astype(f32)
    partial_rewards = jnp.sum(attended * gate * readout, axis=(1, 2)) / math.sqrt(total)
    rewards = lax.psum(jnp.sum(owner * partial_rewards[:, None], axis=0), ("seq", "mp", "section"))
    chosen = (pairs[:, :, None] == jnp.arange(all_cands, dtype=jnp.int32)[None, None, :]).astype(
        f32
    )
    paired = jnp.sum(chosen * rewards[None, None, :], axis=-1)
    margin = paired[:, 0] - paired[:, 1]
    target = labels.astype(f32)
    loss = jnp.sum(jax.nn.softplus(margin) - target * margin)
    coeff = jax.nn.sigmoid(margin) - target
    reward_grad = jnp.sum(coeff[:, None] * (chosen[:, 0] - chosen[:, 1]), axis=0)
    own_grad = jnp.sum(owner * reward_grad[None, :], axis=1)
    upstream = (own_grad[:, None, None] * readout * gate).astype(bf16)
    upstream4 = upstream.reshape(cand, frames_dev, heads_here, HD)
    delta = jnp.sum(upstream4.astype(f32) * attended4, axis=-1).transpose(0, 2, 1)

    def backward_block(start, size):
        prob = weights_for(start, size)
        prob_low = prob.astype(bf16)
        dprob = jnp.einsum(
            "cfhe,ckhe->chfk", upstream4, key_slice(values, start, size), preferred_element_type=f32
        )
        dscore = (prob * (dprob - delta[..., None])).astype(bf16)
        dquery = (
            jnp.einsum(
                "chfk,ckhe->cfhe", dscore, key_slice(keys, start, size), preferred_element_type=f32
            )
            * scale
        )
        dkey = jnp.einsum("chfk,cfhe->kche", dscore, query4, preferred_element_type=f32) * scale
        dvalue = jnp.einsum("chfk,cfhe->kche", prob_low, upstream4, preferred_element_type=f32)
        term = jnp.concatenate(
            [dkey.reshape(size, cand, local_width), dvalue.reshape(size, cand, local_width)],
            axis=-1,
        )
        return (dquery, term)

    zero_query = jnp.zeros((cand, frames_dev, heads_here, HD), f32)

    def grad_step(running, index):
        dquery, term = backward_block(index * block, block)
        return (running + dquery, term.astype(bf16))

    grad_query, stored = lax.scan(grad_step, zero_query, jnp.arange(count_blocks))
    stacked = stored.reshape(total, cand, 2 * local_width)
    summed = lax.psum_scatter(
        stacked.astype(f32).astype(jnp.bfloat16), "seq", scatter_dimension=0, tiled=True
    ).astype(jnp.float32)
    grad_key = summed[:, :, :local_width].transpose(1, 0, 2)
    grad_value = summed[:, :, local_width:].transpose(1, 0, 2)
    grads = jnp.stack(
        [grad_query.reshape(cand, frames_dev, local_width), grad_key, grad_value], axis=0
    ).astype(bf16)
    return (grads, rewards, loss.reshape(1))


def solution(mesh):
    placed = (
        P(("groups", "section"), "mp", "seq"),
        P("mp"),
        P("mp", None, None),
        P(None, None, "mp"),
        P("mp"),
        P(("groups", "section")),
        P("groups", None),
        P("groups"),
    )
    return jax.shard_map(
        local,
        mesh=mesh,
        in_specs=placed,
        out_specs=(P(None, ("groups", "section"), "seq", "mp"), P("groups"), P("groups")),
        check_vma=False,
    )
```

profile of v0, /device:TPU:0, one launch (start us, length us, event | category | flops | bytes accessed | tf_op | source)
XLA Modules:
  0.0 278.7 jit_solution(6267920341593110061)
XLA Ops:
  7.2 8.6 %fusion.25 = bf16[1,256,2048]{2,1,0:T(8,128)(2,1)S(1)} fusion(bf16[1,256,2048]{2,1,0:T(8,128)(2,1)} %param.14, f32[256]{0:T(256)} %param.15), kind=kLoop, calls=%fused_computation.40 | loop fusion | flops 3145728 | bytes 2098176 | tf_op jit(solution)/shard_map/convert_element_type | solution.py:49
  15.9 1.0 copy-done.5
  17.0 4.9 %collective-permute-start = (bf16[1,256,4]{2,1,0:T(8,128)(2,1)S(1)}, bf16[1,256,4]{2,1,0:T(8,128)(2,1)S(1)}, u32[]{:S(2)}, u32[]{:S(2)}) collective-permute-start(bf16[1,256,4]{2,1,0:T(8,128)(2,1)S(1)} %get-tuple-element.365), channel_id=1, source_target_pairs={{0,4},{4,8},{8,12},{1,5},{5,9},{9,13},{2,6},{6,10},{10,14},{3,7},{... | collective-permute-start | bytes 6152 | tf_op jit(solution)/shard_map/ppermute | solution.py:21
  21.9 1.5 collective-permute-start.1
  24.1 2.4 reshape.438
  26.5 1.5 collective-permute-done.1
  28.1 3.5 %concatenate.32 = bf16[1,256,2056]{2,1,0:T(8,128)(2,1)} concatenate(bf16[1,256,4]{2,1,0:T(8,128)(2,1)S(1)} %collective-permute-done, bf16[1,256,2048]{2,1,0:T(8,128)(2,1)} %copy-done.5, bf16[1,256,4]{2,1,0:T(8,128)(2,1)S(1)} %collective-permute-done.1), dimensions={2} | concatenate | bytes 2105344 | tf_op jit(solution)/shard_map/concatenate | solution.py:25
  31.6 2.3 copy.41
  33.9 5.8 %reshape.436 = bf16[1,8,32,257,8]{2,1,4,3,0:T(8,128)(2,1)} reshape(bf16[1,256,2056]{1,2,0:T(8,128)(2,1)} %copy.41) | data formatting | bytes 2105344 | tf_op jit(solution)/shard_map/reshape | solution.py:51
  39.7 6.5 %fusion.53 = (bf16[1,8,256,32,8]{3,1,4,2,0:T(8,128)(2,1)}, bf16[1,8,256,32,8]{3,1,4,2,0:T(8,128)(2,1)}) fusion(bf16[1,8,257,32,8]{3,1,4,2,0:T(8,128)(2,1)} %bitcast.233), kind=kLoop, calls=%fused_computation.102 | loop fusion | bytes 4194304 | tf_op jit(solution)/shard_map/slice | solution.py:54
  46.2 7.7 %copy.42 = bf16[1,8,256,32,8]{2,4,3,1,0:T(8,128)(2,1)} copy(bf16[1,8,256,32,8]{3,1,4,2,0:T(8,128)(2,1)} %get-tuple-element.362) | data formatting | bytes 2097152 | tf_op jit(solution)/shard_map/slice | solution.py:54
  53.9 7.7 %copy.43 = bf16[1,8,256,32,8]{2,4,3,1,0:T(8,128)(2,1)} copy(bf16[1,8,256,32,8]{3,1,4,2,0:T(8,128)(2,1)} %get-tuple-element.363) | data formatting | bytes 2097152 | tf_op jit(solution)/shard_map/slice | solution.py:54
  61.7 1.8 pad_maximum_fusion
  63.5 1.3 fusion.27
  64.9 2.0 copy.46
  66.9 3.5 %fusion.31 = bf16[1,256,512]{2,1,0:T(8,128)(2,1)S(1)} fusion(f32[1,256,512]{2,1,0:T(8,128)} %copy.46, f32[512]{0:T(512)S(1)} %fusion.36, f32[256]{0:T(256)S(1)} %add_convert_fusion, pred[512]{0:T(512)(128)(4,1)S(1)} %fusion.33), kind=kLoop, calls=%fused_computation.52 | loop fusion | flops 524288 | bytes 790016 | tf_op jit(solution)/shard_map/convert_element_type | solution.py:67
  71.1 7.3 %all_gather.9 = bf16[1,256,1024]{2,1,0:T(8,128)(2,1)S(1)} all-gather(bf16[1,256,512]{2,1,0:T(8,128)(2,1)S(1)} %fusion.31), channel_id=1, replica_groups=mesh['groups'=2,'seq'=4,'mp'=2,'section'=2] {'mp'}, dimensions={2}, use_global_device_ids=true | all-gather | bytes 786432 | tf_op jit(solution)/shard_map/all_gather | solution.py:68
  78.6 1.0 fusion.26
  79.6 0.9 fusion.55
  80.7 1.1 copy.47
  82.1 28.3 %all-gather.5.cloned.1.call-done = bf16[1,1024,1,512]{3,1,2,0:T(8,128)(2,1)} async-done(((bf16[1,256,1,512]{3,1,2,0:T(8,128)(2,1)}), bf16[1,1024,1,512]{3,1,2,0:T(8,128)(2,1)}) %all-gather.5.cloned.1.call-update) | async-done | bytes 1048592 | tf_op jit(solution)/shard_map/all_gather | solution.py:74
  110.4 2.3 copy.53
  112.6 16.1 %while.37 = (s32[]{:T(128)}, f32[1,8,256]{2,1,0:T(8,128)S(1)}, f32[1,8,256]{2,1,0:T(8,128)S(1)}, s32[2]{0:T(128)S(1)}, bf16[1,1024,512]{1,2,0:T(8,128)(2,1)}, /*...) while((s32[]{:T(128)}, f32[1,8,256]{2,1,0:T(8,128)S(1)}, ...), condition=%wide.region_4.5_spmd.clone, body=%wide.region_1.4_spmd.clone.sunk | while | flops 139470848 | bytes 10330286 | solution.py:104
  113.9 1.1 constant_dynamic-slice_fusion.8
  115.0 2.7 bitcast_reduce_fusion.2
  117.7 3.0 %fusion.86 = f32[8,256]{1,0:T(8,128)S(1)} fusion(f32[8,512,256]{2,1,0:T(8,128)} %get-tuple-element.514, f32[8,256]{1,0:T(8,128)S(1)} %bitcast.239), kind=kLoop, calls=%fused_computation.3.clone.1 | loop fusion | flops 3143680 | bytes 4210688 | tf_op jit(solution)/shard_map/while/body/eval_jaxpr/reduce_sum | solution.py:98
  122.0 1.1 constant_dynamic-slice_fusion.8
  123.1 2.7 bitcast_reduce_fusion.2
  125.8 2.9 %fusion.86 = f32[8,256]{1,0:T(8,128)S(1)} fusion(f32[8,512,256]{2,1,0:T(8,128)} %get-tuple-element.514, f32[8,256]{1,0:T(8,128)S(1)} %bitcast.239), kind=kLoop, calls=%fused_computation.3.clone.1 | loop fusion | flops 3143680 | bytes 4210688 | tf_op jit(solution)/shard_map/while/body/eval_jaxpr/reduce_sum | solution.py:98
  128.7 10.6 %all-gather.7.cloned.1.call-done = bf16[1,1024,1,512]{3,1,2,0:T(8,128)(2,1)} async-done(((bf16[1,256,1,512]{3,1,2,0:T(8,128)(2,1)}), bf16[1,1024,1,512]{3,1,2,0:T(8,128)(2,1)}) %all-gather.7.cloned.1.call-update) | async-done | bytes 1048592 | tf_op jit(solution)/shard_map/all_gather | solution.py:75
  139.4 2.3 copy.54
  141.7 13.9 %while.38 = (s32[]{:T(128)}, f32[1,256,8,64]{1,3,2,0:T(8,128)}, s32[2]{0:T(128)S(1)}, bf16[1,1024,512]{1,2,0:T(8,128)(2,1)}, bf16[1,1024,512]{1,2,0:T(8,128)(2,1...) while((s32[]{:T(128)}, f32[1,256,8,64]{1,3,2,0:T(8,128)}, ...), condition=%wide.region_6.7_spmd.clone, body=%wide.region_5.6_spmd.clone.sunk | while | flops 272891904 | bytes 4473021 | solution.py:119
  142.9 2.3 constant_dynamic-slice_fusion.9
  145.2 3.4 %fusion.90 = f32[1,256,8,64]{1,3,2,0:T(8,128)} fusion(bf16[512,8,64]{0,2,1:T(8,128)(2,1)} %bitcast.236, bf16[512,8,64]{0,2,1:T(8,128)(2,1)} %bitcast.235, f32[8,256]{1,0:T(8,128)S(1)} %bitcast.249, f32[8,256]{1,0:T(8,128)S(1)} %bitcast.245, f32[1,256,8,64]{1,3,2,0:T(8,128)} %get-tuple-element.581, ...), kind=kOutput, calls=%fused_computation.13.clone.1 | convolution fusion | flops 272891904 | bytes 2375681 | tf_op jit(solution)/shard_map/while/body/eval_jaxpr/chfk,ckhe->cfhe/dot_general | solution.py:114
  149.8 2.3 constant_dynamic-slice_fusion.9
  152.0 3.6 %fusion.90 = f32[1,256,8,64]{1,3,2,0:T(8,128)} fusion(bf16[512,8,64]{0,2,1:T(8,128)(2,1)} %bitcast.236, bf16[512,8,64]{0,2,1:T(8,128)(2,1)} %bitcast.235, f32[8,256]{1,0:T(8,128)S(1)} %bitcast.249, f32[8,256]{1,0:T(8,128)S(1)} %bitcast.245, f32[1,256,8,64]{1,3,2,0:T(8,128)} %get-tuple-element.581, ...), kind=kOutput, calls=%fused_computation.13.clone.1 | convolution fusion | flops 272891904 | bytes 2375681 | tf_op jit(solution)/shard_map/while/body/eval_jaxpr/chfk,ckhe->cfhe/dot_general | solution.py:114
  155.6 2.1 copy.51
  157.7 1.9 multiply_reduce_fusion.2
  160.3 31.9 %psum.7 = f32[2]{0:T(128)S(1)} all-reduce(f32[2]{0:T(128)S(1)} %compare_select_fusion.2), channel_id=1, replica_groups=mesh['groups'=2,'seq'=4,'mp'=2,'section'=2] {'seq','mp','section'}, use_global_device_ids=true, to_apply=%region_8.9 | all-reduce | flops 2 | bytes 16 | tf_op jit(solution)/shard_map/psum | solution.py:131
  194.3 1.8 multiply_convert_fusion.2
  196.1 1.1 copy.52
  197.1 1.1 multiply_reduce_fusion.1
  198.3 25.0 %while.39 = (s32[]{:T(128)}, f32[1,256,8,64]{1,3,2,0:T(8,128)}, bf16[2,512,1,1024]{1,3,2,0:T(8,128)(2,1)}, s32[2]{0:T(128)S(1)}, bf16[1,1024,512]{1,2,0:T(8,128)...) while((s32[]{:T(128)}, f32[1,256,8,64]{1,3,2,0:T(8,128)}, ...), condition=%wide.region_14.15_spmd.clone, body=%wide.region_13.14_spmd.clone.sunk | while | flops 681705472 | bytes 39346984 | solution.py:173
  199.5 1.3 constant_dynamic-slice_fusion.10
  200.8 2.2 exponential_divide_fusion.2
  203.0 0.8 multiply_convert_fusion.4
  203.8 1.3 copy-done.1
  205.2 0.8 fusion.103
  205.9 0.8 fusion.102
  206.7 1.0 maximum_dynamic-update-slice_fusion.2
  207.7 3.0 %fusion.101 = f32[1,256,8,64]{1,3,2,0:T(8,128)} fusion(bf16[512,8,64]{0,2,1:T(8,128)(2,1)} %bitcast.227, bf16[8,512,256]{2,1,0:T(8,128)(2,1)} %copy-done.1, f32[1,256,8,64]{1,3,2,0:T(8,128)} %get-tuple-element.620, pred[]{:T(512)S(6)} %compare.19), kind=kOutput, calls=%fused_computation.27.clone.1 | convolution fusion | flops 134610944 | bytes 3670017 | tf_op jit(solution)/shard_map/while/body/eval_jaxpr/chfk,ckhe->cfhe/dot_general | solution.py:154
  212.0 1.3 constant_dynamic-slice_fusion.10
  213.3 2.2 exponential_divide_fusion.2
  215.5 0.8 multiply_convert_fusion.4
  216.3 1.3 copy-done.1
  218.4 0.8 fusion.102
  219.1 1.1 maximum_dynamic-update-slice_fusion.2
  220.2 3.1 %fusion.101 = f32[1,256,8,64]{1,3,2,0:T(8,128)} fusion(bf16[512,8,64]{0,2,1:T(8,128)(2,1)} %bitcast.227, bf16[8,512,256]{2,1,0:T(8,128)(2,1)} %copy-done.1, f32[1,256,8,64]{1,3,2,0:T(8,128)} %get-tuple-element.620, pred[]{:T(512)S(6)} %compare.19), kind=kOutput, calls=%fused_computation.27.clone.1 | convolution fusion | flops 134610944 | bytes 3670017 | tf_op jit(solution)/shard_map/while/body/eval_jaxpr/chfk,ckhe->cfhe/dot_general | solution.py:154
  223.3 3.3 %copy.58 = bf16[2,1,128,8,512]{4,3,0,2,1:T(8,128)(2,1)} copy(bf16[2,1,128,8,512]{4,3,2,1,0:T(8,128)(2,1)} %bitcast.70) | data formatting | bytes 4194304 | tf_op jit(solution)/shard_map/reshape | solution.py:174
  226.6 1.1 convert.27
  227.7 40.2 %reduce-scatter.2.cloned.1.call-done = bf16[256,1,1024]{0,2,1:T(8,128)(2,1)} async-done(((bf16[1024,1,1024]{0,2,1:T(8,128)(2,1)}), bf16[256,1,1024]{0,2,1:T(8,128)(2,1)}) %reduce-scatter.2.cloned.1.call-update) | async-done | bytes 524304 | tf_op jit(solution)/shard_map/reduce_scatter | solution.py:175
  267.8 1.1 slice_bitcast_fusion.1
  268.9 1.0 pad_maximum_fusion.1
  269.9 2.3 copy.56
  (68 shorter events, 8.0 us)
Async XLA Ops:
  7.2 71.4 %copy-start = (bf16[1024,3,512]{2,0,1:T(8,128)(2,1)S(1)}, bf16[1024,3,512]{2,0,1:T(8,128)(2,1)}, u32[]{:S(2)}) copy-start(bf16[1024,3,512]{2,0,1:T(8,128)(2,1)} %param.17) | copy-start | bytes 9437188
  7.2 103.2 %all-gather.5.cloned.1.call-start = ((), (), s32[]{:S(2)}) async-start(), calls=%async_computation.2 | async-start | bytes 1310720 | tf_op jit(solution)/shard_map/all_gather | solution.py:74
  15.8 1.0 copy-start.5
  17.0 9.6 %collective-permute-start = (bf16[1,256,4]{2,1,0:T(8,128)(2,1)S(1)}, bf16[1,256,4]{2,1,0:T(8,128)(2,1)S(1)}, u32[]{:S(2)}, u32[]{:S(2)}) collective-permute-start(bf16[1,256,4]{2,1,0:T(8,128)(2,1)S(1)} %get-tuple-element.365), channel_id=1, source_target_pairs={{0,4},{4,8},{8,12},{1,5},{5,9},{9,13},{2,6},{6,10},{10,14},{3,7},{... | collective-permute-start | bytes 6152 | tf_op jit(solution)/shard_map/ppermute | solution.py:21
  21.9 6.2 %collective-permute-start.1 = (bf16[1,256,4]{2,1,0:T(8,128)(2,1)S(1)}, bf16[1,256,4]{2,1,0:T(8,128)(2,1)S(1)}, u32[]{:S(2)}, u32[]{:S(2)}) collective-permute-start(bf16[1,256,4]{2,1,0:T(8,128)(2,1)S(1)} %get-tuple-element.364), channel_id=1, source_target_pairs={{4,0},{8,4},{12,8},{5,1},{9,5},{13,9},{6,2},{10,6},{14,10},{7,3},{... | collective-permute-start | bytes 6152 | tf_op jit(solution)/shard_map/ppermute | solution.py:24
  61.7 1.9 copy-start.6
  70.4 0.7 copy-start.7
  78.6 2.1 copy-start.9
  80.6 58.8 %all-gather.7.cloned.1.call-start = ((), (), s32[]{:S(2)}) async-start(), calls=%async_computation.3 | async-start | bytes 1310720 | tf_op jit(solution)/shard_map/all_gather | solution.py:75
  81.8 186.0 %reduce-scatter.2.cloned.1.call-start = ((), (), s32[]{:S(2)}) async-start(), calls=%async_computation.1 | async-start | bytes 2621440 | tf_op jit(solution)/shard_map/reduce_scatter | solution.py:175
  141.7 16.1 %copy-start.8 = (f32[512]{0:T(512)S(1)}, f32[512]{0:T(512)}, u32[]{:S(2)}) copy-start(f32[512]{0:T(512)} %param.18) | copy-start | bytes 6148
  141.7 50.6 %copy-start.10 = (s32[4]{0:T(128)S(1)}, s32[4]{0:T(128)}, u32[]{:S(2)}) copy-start(s32[4]{0:T(128)} %param.21) | copy-start | bytes 52
  155.6 38.7 %copy-start.3 = (bf16[1,256,8,64]{1,3,2,0:T(8,128)(2,1)}, bf16[1,256,8,64]{1,3,2,0:T(8,128)(2,1)S(1)}, u32[]{:S(2)}) copy-start(bf16[1,256,8,64]{1,3,2,0:T(8,128)(2,1)S(1)} %get-tuple-element.656) | copy-start | bytes 786436
  192.2 6.1 %copy-start.11 = (f32[2]{0:T(128)}, f32[2]{0:T(128)S(1)}, u32[]{:S(2)}) copy-start(f32[2]{0:T(128)S(1)} %psum.7) | copy-start | bytes 28
  200.8 2.2 copy-start.2
  203.0 2.1 copy-start.4
  203.8 1.3 copy-start.1
  213.3 2.2 copy-start.2
  215.5 2.1 copy-start.4
  216.3 1.3 copy-start.1
Sparse Core Ops, SparseCore 0:
  80.7 29.6 all-gather.4
  111.9 27.4 all-gather.6
  226.7 41.0 reduce-scatter.1
where the time goes:
time: 280 us; the launch traced here: 279 us
  waiting for transfers between devices  80.7 us (29%)
  local copies, waits for them, and re-layouts  71.9 us (26%)
  blocking collectives  39.2 us (14%)
  other arithmetic  31.1 us (11%)
  matrix products  29.7 us (11%)
  between operations  15.3 us (5%)
  starting transfers between devices  6.74 us (2%)
  loops' own time  4.08 us (1%)
    reduce_scatter x1, waiting for transfers between devices, local(): lax.psum_scatter(stacked.astype(f32).astype(jnp.bfloat16), 'seq', scatter...  40.2 us
    psum x1, blocking collectives, local(): lax.psum(jnp.sum(owner * partial_rewards[:, None], axis=0), ('seq', 'mp',...  31.9 us
    all_gather x1, waiting for transfers between devices, local(): lax.all_gather(qkv[:, :, 1], 'seq', axis=1, tiled=True)  28.3 us
    slice x2, local copies, waits for them, and re-layouts, local(): blocks[:, :, :-1]  14.2 us
    all_gather x1, waiting for transfers between devices, local(): lax.all_gather(qkv[:, :, 2], 'seq', axis=1, tiled=True)  10.6 us
    dot_general x4, matrix products, scores_for(): jnp.einsum('cfhe,ckhe->chfk', query4, key_slice(keys, start, size), prefe...  9.74 us
    dynamic_slice x6, local copies, waits for them, and re-layouts, key_slice(): lax.dynamic_slice_in_dim(source, start, size, 1)  9.22 us
    unnamed x21, local copies, waits for them, and re-layouts  8.64 us
  transfers between devices with their start and end apart: 5, of which 4 were waited for; matrix products, arithmetic and copies ran while one was open for 8% of the time, Pallas kernels for 0%

commit v1 on v0

--- a/solution.py
+++ b/solution.py
@@ -2,7 +2,10 @@
 
 import jax
 import jax.numpy as jnp
+import numpy as np
 from jax import lax
+from jax.experimental import pallas as pl
+from jax.experimental.pallas import tpu as pltpu
 from jax.sharding import PartitionSpec as P
 
 D = 1024
@@ -183,6 +186,409 @@
     return (grads, rewards, loss.reshape(1))
 
 
+PI_PARTS = (3.140625, 0.0009670257568359375, 6.2771141529083251953e-07, 1.2154201256553420762e-10)
+SIN_COEFFS = (-1.0 / 6, 1.0 / 120, -1.0 / 5040, 1.0 / 362880, -1.0 / 39916800)
+
+
+def reduced_sin(angle, turns, parts):
+    for part in PI_PARTS[:parts]:
+        angle = angle - turns * part
+    square = angle * angle
+    poly = jnp.full_like(square, SIN_COEFFS[-1])
+    for coeff in SIN_COEFFS[-2::-1]:
+        poly = poly * square + coeff
+    return angle + angle * square * poly
+
+
+def snake(raw, slope, inverse):
+    angle = slope * raw
+    sine = reduced_sin(angle, jnp.round(angle * (1.0 / math.pi)), 3)
+    return (raw + sine * sine * inverse).astype(jnp.bfloat16)
+
+
+def nn(a, b):
+    return jnp.dot(a, b, preferred_element_type=jnp.float32)
+
+
+def nt(a, b):
+    return lax.dot_general(a, b, (((1,), (1,)), ((), ())), preferred_element_type=jnp.float32)
+
+
+def fused_kernel(n_seq, n_mp, n_sec):
+    f32 = jnp.float32
+    bf16 = jnp.bfloat16
+
+    def kernel(
+        feats, alpha, conv_w, qkv_w, readout, freqs, offsets, pairs, labels,
+        grads, rewards_out, loss_out,
+        halo, act0, act1, conv_f, conv_b, patches, weights, whole, resid_out, resid_in,
+        qkv_out, qkv_in, prob, up_m, q_m, delta, gq_sum, reward_slots, grad_out,
+        halo_sem, mp_sem, weight_sem, resid_sem, qkv_sem, reward_sem, grad_sem,
+    ):
+        me = lax.axis_index("seq")
+        part = lax.axis_index("mp")
+        sec = lax.axis_index("section")
+        other = 1 - part
+        chans, samples = feats.shape
+        taps = conv_w.shape[1]
+        per_group = conv_w.shape[0]
+        width = conv_w.shape[2]
+        stride = taps // 2
+        fr = samples // stride
+        cols = width // n_seq
+        total = fr * n_seq
+
+        def remote(src, dst, sems, send, recv, **where):
+            return pltpu.make_async_remote_copy(
+                src_ref=src, dst_ref=dst, send_sem=sems.at[0].at[send], recv_sem=sems.at[1].at[recv],
+                device_id=where, device_id_type=pl.DeviceIdType.MESH,
+            )
+
+        weight_copy = pltpu.make_async_copy(qkv_w, weights, weight_sem)
+        weight_copy.start()
+        barrier = pltpu.get_barrier_semaphore()
+        peers = [
+            (a, b, c) for a in range(n_seq) for b in range(n_mp) for c in range(n_sec) if (a, b, c) != (0, 0, 0)
+        ]
+
+        def peer(step):
+            return dict(
+                seq=lax.rem(me + step[0], n_seq),
+                mp=lax.rem(part + step[1], n_mp),
+                section=lax.rem(sec + step[2], n_sec),
+            )
+
+        for step in peers:
+            pl.semaphore_signal(barrier, inc=1, device_id=peer(step), device_id_type=pl.DeviceIdType.MESH)
+        pl.semaphore_wait(barrier, len(peers))
+
+        to_right = remote(feats.at[:, samples - 128 : samples], halo.at[0], halo_sem, 0, 0, seq=lax.rem(me + 1, n_seq))
+        to_left = remote(feats.at[:, 0:128], halo.at[1], halo_sem, 1, 1, seq=lax.rem(me + n_seq - 1, n_seq))
+
+        @pl.when(me < n_seq - 1)
+        def _():
+            to_right.start()
+
+        @pl.when(me > 0)
+        def _():
+            to_left.start()
+
+        slope = alpha[...]
+        inverse = 1.0 / slope
+
+        def put_act(row, block):
+            act0[pl.ds(row, block.shape[0]), :] = block[:, :128]
+            act1[pl.ds(row, block.shape[0]), :] = block[:, 128:]
+
+        def act_step(i, carry):
+            raw = feats[:, pl.ds(pl.multiple_of(i * 256, 256), 256)].astype(f32).T
+            put_act(pl.multiple_of(8 + i * 256, 8), snake(raw, slope, inverse).astype(f32))
+            return carry
+
+        lax.fori_loop(0, samples // 256, act_step, 0)
+
+        for j in range(width // 128):
+            conv_f[j] = conv_w[:, :, j * 128 : (j + 1) * 128].astype(f32).reshape(per_group * taps, 128)
+        group_out = width // (chans // per_group)
+        for j in range(width // 128):
+            rows = lax.broadcasted_iota(jnp.int32, (chans, 128), 0) // per_group
+            outs = (lax.broadcasted_iota(jnp.int32, (chans, 128), 1) + j * 128) // group_out
+            for t in range(taps):
+                tap = conv_f.at[j][pl.ds(t, per_group, stride=taps), :]
+                tiled = jnp.concatenate([tap] * (chans // per_group), axis=0)
+                conv_b[t * chans : (t + 1) * chans, j * 128 : (j + 1) * 128] = jnp.where(rows == outs, tiled, 0.0).astype(bf16)
+
+        feature = lax.broadcasted_iota(jnp.int32, (1, width), 1)
+        odd = (feature - 2 * (feature // 2)).astype(f32)
+        spots = (offsets[0] + me * fr + lax.broadcasted_iota(jnp.int32, (fr, 1), 0)).astype(f32)
+        angle = spots * freqs[:, pl.ds(pl.multiple_of(part * width, 128), width)]
+        whole_turns = jnp.round(angle * (1.0 / math.pi) - 0.5 * odd)
+        sine = reduced_sin(angle, whole_turns + 0.5 * odd, 4)
+        signed = whole_turns + odd
+        parity = signed - 2.0 * jnp.floor(signed * 0.5)
+        table = sine * (1.0 - 2.0 * parity)
+
+        @pl.when(me < n_seq - 1)
+        def _():
+            to_right.wait_send()
+            to_left.wait_recv()
+            put_act(8 + samples, snake(halo[1].astype(f32).T[:8], slope, inverse).astype(f32))
+
+        @pl.when(me == n_seq - 1)
+        def _():
+            put_act(8 + samples, jnp.zeros((8, chans), f32))
+
+        @pl.when(me > 0)
+        def _():
+            to_left.wait_send()
+            to_right.wait_recv()
+            put_act(0, snake(halo[0].astype(f32).T[120:], slope, inverse).astype(f32))
+
+        @pl.when(me == 0)
+        def _():
+            put_act(0, jnp.zeros((8, chans), f32))
+
+        for t in range(taps):
+            first = 8 - stride // 2 + t
+            patches[:, t * chans : t * chans + 128] = act0[pl.ds(first, fr, stride=stride), :].astype(bf16)
+            patches[:, t * chans + 128 : (t + 1) * chans] = act1[pl.ds(first, fr, stride=stride), :].astype(bf16)
+        resid = (nn(patches[...], conv_b[...]) + table).astype(bf16)
+
+        whole[part] = resid
+        to_mp = remote(whole.at[part], whole.at[part], mp_sem, 0, 0, mp=other)
+        to_mp.start()
+        for z in range(n_seq):
+            resid_out[z] = resid[:, z * cols : (z + 1) * cols]
+        resid_in[me] = resid_out[me]
+        sent = []
+        for d in range(1, n_seq):
+            z = lax.rem(me + d, n_seq)
+            copy = remote(resid_out.at[z], resid_in.at[me], resid_sem, z, me, seq=z)
+            copy.start()
+            sent.append(copy)
+        wide = resid.astype(f32)
+        squares = jnp.sum(wide * wide, axis=1, keepdims=True)
+        own_rows = pl.ds(pl.multiple_of(part * width, 128), width)
+        other_rows = pl.ds(pl.multiple_of(other * width, 128), width)
+        weight_copy.wait()
+        halves = [nn(resid, weights[t, own_rows, :]) for t in range(3)]
+        from_mp = remote(whole.at[other], whole.at[other], mp_sem, 0, 0, mp=other)
+        from_mp.wait_recv()
+        rest = whole[other]
+        wide = rest.astype(f32)
+        squares = squares + jnp.sum(wide * wide, axis=1, keepdims=True)
+        norm = lax.rsqrt(squares * (1.0 / (width * n_mp)) + EPS)
+        for t in (1, 2, 0):
+            value = ((halves[t] + nn(rest, weights[t, other_rows, :])) * norm).astype(bf16)
+            if t == 0:
+                value = value * jnp.asarray(1.0 / math.sqrt(HD), bf16)
+            for z in range(n_seq):
+                qkv_out[t, z] = value[:, z * cols : (z + 1) * cols]
+            qkv_in[t, me] = qkv_out[t, me]
+            for d in range(1, n_seq):
+                z = lax.rem(me + d, n_seq)
+                copy = remote(qkv_out.at[t, z], qkv_in.at[t, me], qkv_sem.at[t], z, me, seq=z)
+                copy.start()
+                sent.append(copy)
+
+        def arrive(ref, sems):
+            for d in range(1, n_seq):
+                z = lax.rem(me + d, n_seq)
+                remote(ref.at[z], ref.at[z], sems, z, z, seq=z).wait_recv()
+
+        heads = cols // HD
+        row_head = lax.broadcasted_iota(jnp.int32, (cols, 1), 0) // HD
+        lane_head = lax.broadcasted_iota(jnp.int32, (1, cols), 1) // HD
+
+        def rows_of(value, h):
+            return jnp.where(row_head == h, value, jnp.zeros_like(value))
+
+        def lanes_of(value, h):
+            return jnp.where(lane_head == h, value, jnp.zeros_like(value))
+
+        def flipped(value):
+            return value.astype(f32).T.astype(bf16)
+
+        arrive(resid_in, resid_sem)
+        read = jnp.broadcast_to(readout[pl.ds(me, 1), :], (cols, cols)).T[:, :1]
+        for z in range(n_seq):
+            up = jax.nn.sigmoid(resid_in[z].astype(f32).T) * read
+            gq_sum[:, z * fr : (z + 1) * fr] = up
+            for h in range(heads):
+                up_m[h, :, z * fr : (z + 1) * fr] = rows_of(up, h).astype(bf16)
+        for t in (1, 2, 0):
+            arrive(qkv_in.at[t], qkv_sem.at[t])
+
+        keys = qkv_in[1].reshape(total, cols)
+        values_t = flipped(qkv_in[2].reshape(total, cols))
+        for h in range(heads):
+            q_m[h] = lanes_of(qkv_in[0].reshape(total, cols), h)
+        values_h = [rows_of(values_t, h) for h in range(heads)]
+
+        def forward(c, carry):
+            chunk = pl.ds(pl.multiple_of(c * fr, fr), fr)
+            attended = jnp.zeros((cols, fr), f32)
+            for h in range(heads):
+                score = nt(keys, q_m[h, chunk, :])
+                weight = jnp.exp(score - jnp.max(score, axis=0, keepdims=True))
+                share = weight * (1.0 / jnp.sum(weight, axis=0, keepdims=True))
+                prob[h, :, chunk] = share
+                out = nn(values_h[h], share.astype(bf16))
+                delta[h : h + 1, chunk] = jnp.sum(out * up_m[h, :, chunk].astype(f32), axis=0, keepdims=True)
+                attended = attended + out
+            return carry + attended * gq_sum[:, chunk]
+
+        reward = lax.fori_loop(0, n_seq, forward, jnp.zeros((cols, fr), f32))
+        own = (me * n_mp + part) * n_sec + sec
+        reward_slots[own] = jnp.full((8, 128), jnp.sum(reward), f32)
+        for step in peers:
+            where = peer(step)
+            index = (step[0] * n_mp + step[1]) * n_sec + step[2]
+            copy = remote(reward_slots.at[own], reward_slots.at[own], reward_sem, index, own, **where)
+            copy.start()
+            sent.append(copy)
+
+        gq_sum[...] = jnp.zeros_like(gq_sum)
+        gain = None
+        for d in list(range(1, n_seq)) + [0]:
+            z = lax.rem(me + d, n_seq)
+            rows = pl.ds(pl.multiple_of(z * fr, fr), fr)
+            key_t = flipped(qkv_in[1, z]) * jnp.asarray(1.0 / math.sqrt(HD), bf16)
+            grad_k = jnp.zeros((fr, cols), f32)
+            grad_v = jnp.zeros((fr, cols), f32)
+            for h in range(heads):
+                share = prob[h, rows, :]
+                dprob = nn(qkv_in[2, z], up_m[h])
+                dscore = (share * (dprob - delta[h : h + 1, :])).astype(bf16)
+                grad_k = grad_k + nn(dscore, q_m[h])
+                grad_v = grad_v + nt(share.astype(bf16), up_m[h])
+                gq_sum[...] += nn(rows_of(key_t, h), dscore)
+            if gain is None:
+                for step in peers:
+                    where = peer(step)
+                    index = (where["seq"] * n_mp + where["mp"]) * n_sec + where["section"]
+                    remote(reward_slots.at[index], reward_slots.at[index], reward_sem, 0, index, **where).wait_recv()
+                rewards = []
+                for c in range(n_sec):
+                    one = reward_slots[c]
+                    for k in range(1, n_seq * n_mp):
+                        one = one + reward_slots[k * n_sec + c]
+                    one = one * (1.0 / math.sqrt(total))
+                    rewards.append(one)
+                    rewards_out[c] = jnp.max(one)
+                loss = jnp.zeros((8, 128), f32)
+                gain = jnp.zeros((8, 128), f32)
+                for p in range(labels.shape[0]):
+                    picks = [pairs[p, 0], pairs[p, 1]]
+                    sides = []
+                    for pick in picks:
+                        flag = pick.astype(f32)
+                        sides.append(rewards[0] * (1.0 - flag) + rewards[1] * flag)
+                    margin = sides[0] - sides[1]
+                    target = labels[p].astype(f32)
+                    loss = loss + jnp.maximum(margin, 0.0) + jnp.log1p(jnp.exp(-jnp.abs(margin))) - target * margin
+                    mine = (1 - jnp.abs(picks[0] - sec)) - (1 - jnp.abs(picks[1] - sec))
+                    gain = gain + (jax.nn.sigmoid(margin) - target) * mine.astype(f32)
+                loss_out[0] = jnp.max(loss)
+                gain = gain[:1, :1]
+            pieces = ((1, grad_k), (2, grad_v))
+            for t, piece in pieces:
+                scaled = (piece * gain).astype(bf16)
+                if d == 0:
+                    grads[t, :, pl.ds(pl.multiple_of(me * cols, cols), cols)] = scaled
+                else:
+                    grad_out[t, d] = scaled
+                    copy = remote(
+                        grad_out.at[t, d], grads.at[t, :, pl.ds(pl.multiple_of(me * cols, cols), cols)],
+                        grad_sem.at[t], d, me, seq=z,
+                    )
+                    copy.start()
+                    sent.append(copy)
+        for d in list(range(1, n_seq)) + [0]:
+            z = lax.rem(me + d, n_seq)
+            scaled = (gq_sum[:, pl.ds(pl.multiple_of(z * fr, fr), fr)].T * gain).astype(bf16)
+            if d == 0:
+                grads[0, :, pl.ds(pl.multiple_of(me * cols, cols), cols)] = scaled
+            else:
+                grad_out[0, d] = scaled
+                copy = remote(
+                    grad_out.at[0, d], grads.at[0, :, pl.ds(pl.multiple_of(me * cols, cols), cols)],
+                    grad_sem.at[0], d, me, seq=z,
+                )
+                copy.start()
+                sent.append(copy)
+        for t in (1, 2, 0):
+            for d in range(1, n_seq):
+                z = lax.rem(me + d, n_seq)
+                remote(
+                    grad_out.at[t, d], grads.at[t, :, pl.ds(pl.multiple_of(z * cols, cols), cols)],
+                    grad_sem.at[t], d, z, seq=z,
+                ).wait_recv()
+        to_mp.wait_send()
+        for copy in sent:
+            copy.wait_send()
+
+    return kernel
+
+
+def fused_local(n_seq, n_mp, n_sec):
+    def run(features, alpha, conv_weight, qkv_weight, readout, offsets, pairs, labels):
+        f32 = jnp.float32
+        bf16 = jnp.bfloat16
+        _, chans, samples = features.shape
+        width, per_group, taps = conv_weight.shape
+        fr = samples // (taps // 2)
+        cols = width // n_seq
+        total = fr * n_seq
+        heads = cols // HD
+        powers = np.arange(n_mp * width) // 2 * (-2.0 * math.log(BASE) / (n_mp * width))
+        freqs = jnp.asarray(np.exp(powers)[None, :].astype(np.float32))
+        vmem = pl.BlockSpec(memory_space=pltpu.VMEM)
+        smem = pl.BlockSpec(memory_space=pltpu.SMEM)
+        dma = pltpu.SemaphoreType.DMA
+        grads, rewards, loss = pl.pallas_call(
+            fused_kernel(n_seq, n_mp, n_sec),
+            out_shape=[
+                jax.ShapeDtypeStruct((3, fr, width), bf16),
+                jax.ShapeDtypeStruct((n_sec,), f32),
+                jax.ShapeDtypeStruct((1,), f32),
+            ],
+            in_specs=[vmem, vmem, vmem, pl.BlockSpec(memory_space=pl.ANY), vmem, vmem, smem, smem, smem],
+            out_specs=[vmem, smem, smem],
+            scratch_shapes=[
+                pltpu.VMEM((2, chans, 128), bf16),
+                pltpu.VMEM((samples + 16, 128), f32),
+                pltpu.VMEM((samples + 16, 128), f32),
+                pltpu.VMEM((width // 128, per_group * taps, 128), f32),
+                pltpu.VMEM((taps * chans, width), bf16),
+                pltpu.VMEM((fr, taps * chans), bf16),
+                pltpu.VMEM((3, n_mp * width, width), bf16),
+                pltpu.VMEM((n_mp, fr, width), bf16),
+                pltpu.VMEM((n_seq, fr, cols), bf16),
+                pltpu.VMEM((n_seq, fr, cols), bf16),
+                pltpu.VMEM((3, n_seq, fr, cols), bf16),
+                pltpu.VMEM((3, n_seq, fr, cols), bf16),
+                pltpu.VMEM((heads, total, total), f32),
+                pltpu.VMEM((heads, cols, total), bf16),
+                pltpu.VMEM((heads, total, cols), bf16),
+                pltpu.VMEM((8, total), f32),
+                pltpu.VMEM((cols, total), f32),
+                pltpu.VMEM((n_seq * n_mp * n_sec, 8, 128), f32),
+                pltpu.VMEM((3, n_seq, fr, cols), bf16),
+                dma((2, 2)),
+                dma((2, 1)),
+                dma,
+                dma((2, n_seq)),
+                dma((3, 2, n_seq)),
+                dma((2, n_seq * n_mp * n_sec)),
+                dma((3, 2, n_seq)),
+            ],
+            compiler_params=pltpu.CompilerParams(
+                collective_id=0, has_side_effects=True, vmem_limit_bytes=56 * 2**20
+            ),
+        )(
+            features[0],
+            alpha[None, :],
+            conv_weight.transpose(1, 2, 0),
+            qkv_weight.transpose(1, 0, 2),
+            readout.reshape(n_seq, cols),
+            freqs,
+            offsets,
+            pairs,
+            labels,
+        )
+        return grads[:, None], rewards, loss
+
+    return run
+
+
+def chosen_local(mesh):
+    n_seq, n_mp, n_sec = (mesh.shape[axis] for axis in ("seq", "mp", "section"))
+    if n_mp == 2 and n_sec == 2 and n_mp * n_seq * 128 == D:
+        return fused_local(n_seq, n_mp, n_sec)
+    return local
+
+
 def solution(mesh):
     placed = (
         P(("groups", "section"), "mp", "seq"),
@@ -195,7 +601,7 @@
         P("groups"),
     )
     return jax.shard_map(
-        local,
+        chosen_local(mesh),
         mesh=mesh,
         in_specs=placed,
         out_specs=(P(None, ("groups", "section"), "seq", "mp"), P("groups"), P("groups")),

time: 280 us -> 79.6 us (0.28)
  waiting for transfers between devices: 80.7 us -> 0 us
  Pallas kernels: 0 us -> 71.8 us
  local copies, waits for them, and re-layouts: 71.9 us -> 4.49 us
  blocking collectives: 39.2 us -> 0 us
  other arithmetic: 31.1 us -> 0 us
  matrix products: 29.7 us -> 0 us
  between operations: 15.3 us -> 3.05 us
  starting transfers between devices: 6.74 us -> 0 us
  loops' own time: 4.08 us -> 0 us
    pallas_call x0 -> x1, Pallas kernels: none -> 71.8 us  [run(): pl.pallas_call(fused_kernel(n_seq, n_mp, n_sec), out_shape=[jax.ShapeDtyp...]
    reduce_scatter x1 -> x0, waiting for transfers between devices: 40.2 us -> none  [local(): lax.psum_scatter(stacked.astype(f32).astype(jnp.bfloat16), 'seq', scatter...]
    all_gather x2 -> x0, waiting for transfers between devices: 38.9 us -> none  [the longest x1 28.3 us: local(): lax.all_gather(qkv[:, :, 1], 'seq', axis=1, tiled=True)]
    psum x1 -> x0, blocking collectives: 31.9 us -> none  [local(): lax.psum(jnp.sum(owner * partial_rewards[:, None], axis=0), ('seq', 'mp',...]
    dot_general x16 -> x0, matrix products: 29.7 us -> none  [the longest x4 9.74 us: scores_for(): jnp.einsum('cfhe,ckhe->chfk', query4, key_slice(keys, start, size), prefe...]
    slice x6 -> x0, local copies, waits for them, and re-layouts: 24.1 us -> none  [the longest x2 14.2 us: local(): blocks[:, :, :-1]]
    reshape x5 -> x0, local copies, waits for them, and re-layouts: 15.6 us -> none  [the longest x1 5.79 us: local(): padded.reshape(cand, groups_here, per_group, frames_dev + 1, stride)]
    convert_element_type x5 -> x0, other arithmetic: 13.9 us -> none  [the longest x1 8.61 us: local(): act = (raw + jnp.sin(slope * raw) ** 2 / slope).astype(bf16)]
  transfers between devices with their start and end apart: 5 -> 0, of which waited for: 4 -> 0; matrix products, arithmetic and copies ran while one was open for 8% -> 0% of each run, Pallas kernels for 0% -> 0%
where the time goes in v1:
time: 79.6 us; the launch traced here: 79.4 us
  Pallas kernels  71.8 us (90%)
  local copies, waits for them, and re-layouts  4.49 us (6%)
  between operations  3.05 us (4%)
    pallas_call x1, Pallas kernels, run(): pl.pallas_call(fused_kernel(n_seq, n_mp, n_sec), out_shape=[jax.ShapeDtyp...  71.8 us
    unnamed x3, local copies, waits for them, and re-layouts  4.49 us

profile of v1, /device:TPU:0, one launch (start us, length us, event | category | flops | bytes accessed | tf_op | source)
XLA Modules:
  0.0 79.4 jit_solution(13395020603989825191)
XLA Ops:
  1.3 1.3 %copy.12.pairs = s32[4,2]{1,0:T(4,128)} copy(s32[4,2]{0,1:T(2,128)} %param.15) | data formatting | bytes 64 | tf_op args[6]
  2.6 71.8 %shard_map.112 = (bf16[3,256,512]{2,1,0:T(8,128)(2,1)}, f32[2]{0:T(128)}, f32[1]{0:T(128)}) custom-call(bf16[256,2048]{1,0:T(8,128)(2,1)} %bitcast.9, f32[1,256]{1,0:T(1,128)} %bitcast.13, bf16[32,16,512]{2,1,0:T(8,128)(2,1)} %bitcast.11, bf16[3,1024,512]{2,1,0:T(8,128)(2,1)} %bitcast.8, f32[4,128]{1,0:T(4,128)} %bitcast.12, f32[1,1024]{1,0:T(1,128)} %constant.2.clone.freqs, ...), custom_call_target="tpu_custom_call" | custom-call | tf_op jit(solution)/shard_map/pallas_call | solution.py:529
  74.4 2.1 %copy.18 = bf16[3,1,256,512]{3,2,1,0:T(8,128)(2,1)} copy(bf16[3,1,256,512]{3,2,1,0:T(8,128)(2,1)} %bitcast.10) | data formatting | bytes 1572864
  76.5 1.1 %copy.19 = f32[2]{0:T(128)} copy(f32[2]{0:T(128)} %get-tuple-element.16) | data formatting | bytes 16
